TPU v7x, 256 devices: a whole 4x4x8 slice. The times are simulated.
256 devices in a mesh: adapter: 64 (over x, z, core), tensor: 4 (over y).
Axes of the slice: x: 4, y: 4, z: 8, core: 2. Of those that a mesh axis runs over, the one named last changes fastest.
Arguments:
- activations: bfloat16 [32768, 4096], P('adapter', 'tensor'), may hold values from -6 to 6
- output_gradient: bfloat16 [32768, 4096], P('adapter', 'tensor'), may hold values from -6 to 6
- frozen_weight: bfloat16 [4096, 4096], P(None, 'tensor'), may hold values from -0.09375 to 0.09375
- adapter_down_weight: bfloat16 [8192, 4096], P('adapter', 'tensor'), may hold values from -0.09375 to 0.09375
- adapter_up_weight: bfloat16 [8192, 4096], P('adapter', 'tensor'), may hold values from -0.09375 to 0.09375
- adapter_slot_table: int32 [512], replicated, may hold values from 0 to 511, as said below
- group_adapter_index: int32 [64, 48], P('adapter'), may hold values from 0 to 511, as said below
- group_token_length: int32 [64, 48], P('adapter'), may hold values from 1 to 16, as said below
Outputs:
- input_gradient: bfloat16 [32768, 4096], P('adapter', 'tensor')
- down_grad: float32 [8192, 4096], P('adapter', 'tensor')
- up_grad: float32 [8192, 4096], P('adapter', 'tensor')
Inputs may be any that keep to these rules, and one draw needn't show every extreme that they name: `adapter_slot_table`: a permutation of the slots; slot k lies on adapter index k // 8. `group_adapter_index`: the adapters of one index's groups lie on distinct indices of the adapter axis; on every index one group of exactly 16 tokens uses an adapter stored on one index that is the same for all indices. `group_token_length`: each row sums to 512 and holds a group of exactly 16 tokens.
All inputs are finite; a program needn't handle non-finite values.
Results may differ from a plain program's by a relative error of at most 0.015.
Values may be sent and summed in bfloat16 or wider, within the bound.
A program may use at most 128 MiB of HBM per device.

v0:
```python
import jax
import jax.numpy as jnp
from jax import lax
from jax.sharding import PartitionSpec as P

ADAPTER_RANK = 16
ADP_DEV = 8
adapter_scale = 2.0


def rank_sums(down_part, up_part):
    return (
        lax.psum(down_part.astype(jnp.bfloat16), "tensor").astype(jnp.float32),
        lax.psum(up_part.astype(jnp.bfloat16), "tensor").astype(jnp.float32),
    )


def widen(mask, values):
    return jnp.where(mask[:, :, None], values[:, None, :], jnp.zeros((), values.dtype)).reshape(
        values.shape[0], mask.shape[1] * values.shape[1]
    )


def narrow(wide, mask):
    shaped = wide.reshape(wide.shape[0], mask.shape[1], ADAPTER_RANK)
    return jnp.sum(shaped * mask[:, :, None].astype(jnp.float32), axis=1)


def on_device(
    activations,
    output_gradient,
    frozen_weight,
    adapter_down_weight,
    adapter_up_weight,
    adapter_slot_table,
    group_adapter_index,
    group_token_length,
):
    tok_rows = activations.shape[0]
    devices = lax.axis_size("adapter")
    own_index = lax.axis_index("adapter")
    adapter_count = adapter_slot_table.shape[0]
    lengths = group_token_length[0]
    matched = group_adapter_index[0][:, None] == jnp.arange(adapter_count, dtype=jnp.int32)[None, :]
    group_slot = jnp.sum(jnp.where(matched, adapter_slot_table[None, :], 0), axis=1)
    group_owner = group_slot // ADP_DEV
    group_end = jnp.cumsum(lengths)
    positions = jnp.arange(tok_rows, dtype=jnp.int32)
    tok_group = jnp.sum((positions[:, None] >= group_end[None, :]).astype(jnp.int32), axis=1)
    group_onehot = tok_group[:, None] == jnp.arange(lengths.shape[0], dtype=jnp.int32)[None, :]
    tok_owner = jnp.sum(jnp.where(group_onehot, group_owner[None, :], 0), axis=1)
    gathered = lax.all_gather(jnp.stack([group_slot, lengths])[None], "adapter", axis=0, tiled=True)
    from_mine = gathered[:, 0] // ADP_DEV == own_index
    source_count = jnp.sum(jnp.where(from_mine, gathered[:, 1], 0), axis=1)
    source_local = jnp.sum(jnp.where(from_mine, gathered[:, 0] % ADP_DEV, 0), axis=1)
    source_hot = (source_local[:, None] == jnp.arange(ADP_DEV, dtype=jnp.int32)[None, :]) & (
        source_count > 0
    )[:, None]
    eye_rank = jnp.eye(ADAPTER_RANK, dtype=bool)
    selector = (source_hot[:, None, :, None] & eye_rank[None, :, None, :]).reshape(
        devices * ADAPTER_RANK, ADP_DEV * ADAPTER_RANK
    )
    selected_reduced = selector.astype(jnp.bfloat16)
    outgoing_down = jnp.dot(
        selected_reduced, adapter_down_weight, preferred_element_type=jnp.float32
    ).astype(jnp.bfloat16)
    outgoing_up = jnp.dot(
        selected_reduced, adapter_up_weight, preferred_element_type=jnp.float32
    ).astype(jnp.bfloat16)
    received_down, got_up = (
        lax.all_to_all(outgoing_down, "adapter", split_axis=0, concat_axis=0, tiled=True),
        lax.all_to_all(outgoing_up, "adapter", split_axis=0, concat_axis=0, tiled=True),
    )
    owner_hot = tok_owner[:, None] == jnp.arange(devices, dtype=jnp.int32)[None, :]
    down_wide = lax.dot_general(
        activations, received_down, (((1,), (1,)), ((), ())), preferred_element_type=jnp.float32
    )
    up_wide = lax.dot_general(
        output_gradient, got_up, (((1,), (1,)), ((), ())), preferred_element_type=jnp.float32
    )
    down_proj, up_proj = rank_sums(narrow(down_wide, owner_hot), narrow(up_wide, owner_hot))
    down_spread = widen(owner_hot, down_proj.astype(jnp.bfloat16))
    up_broadcast = widen(owner_hot, up_proj.astype(jnp.bfloat16))
    adapter_term = (
        adapter_scale * jnp.dot(up_broadcast, received_down, preferred_element_type=jnp.float32)
    ).astype(jnp.bfloat16)
    partial_down = adapter_scale * lax.dot_general(
        up_broadcast, activations, (((0,), (0,)), ((), ())), preferred_element_type=jnp.float32
    )
    partial_up = adapter_scale * lax.dot_general(
        down_spread, output_gradient, (((0,), (0,)), ((), ())), preferred_element_type=jnp.float32
    )
    back_down, back_up = (
        lax.all_to_all(
            partial_down.astype(jnp.bfloat16), "adapter", split_axis=0, concat_axis=0, tiled=True
        ).astype(partial_down.dtype),
        lax.all_to_all(
            partial_up.astype(jnp.bfloat16), "adapter", split_axis=0, concat_axis=0, tiled=True
        ).astype(partial_up.dtype),
    )
    select_full = selector.astype(jnp.float32)
    down_grad = lax.dot_general(
        select_full,
        back_down,
        (((0,), (0,)), ((), ())),
        precision=lax.Precision.HIGHEST,
        preferred_element_type=jnp.float32,
    )
    up_grad = lax.dot_general(
        select_full,
        back_up,
        (((0,), (0,)), ((), ())),
        precision=lax.Precision.HIGHEST,
        preferred_element_type=jnp.float32,
    )
    frozen_total_sum = lax.psum_scatter(
        lax.dot_general(
            frozen_weight,
            output_gradient,
            (((1,), (1,)), ((), ())),
            preferred_element_type=jnp.float32,
        ).astype(jnp.bfloat16),
        "tensor",
        scatter_dimension=0,
        tiled=True,
    ).astype(jnp.float32)
    input_gradient = (frozen_total_sum.T + adapter_term.astype(jnp.float32)).astype(jnp.bfloat16)
    return (input_gradient, down_grad, up_grad)


def solution(mesh):
    in_specs = (
        P("adapter", "tensor"),
        P("adapter", "tensor"),
        P(None, "tensor"),
        P("adapter", "tensor"),
        P("adapter", "tensor"),
        P(),
        P("adapter", None),
        P("adapter", None),
    )
    out_specs = (P("adapter", "tensor"), P("adapter", "tensor"), P("adapter", "tensor"))
    return jax.shard_map(
        on_device, mesh=mesh, in_specs=in_specs, out_specs=out_specs, check_vma=False
    )
```

profile of v0, /device:TPU:1, one launch (start us, length us, event | category | flops | bytes accessed | tf_op | source)
XLA Modules:
  0.0 331.1 jit_solution(9683461043637806220)
XLA Ops:
  7.2 1.0 select_reduce_fusion.1
  8.2 0.7 add_bitcast_fusion
  8.8 48.1 %all-gather.1 = s32[64,2,48]{2,1,0:T(2,128)S(1)} all-gather(s32[1,2,48]{2,1,0:T(2,128)S(1)} %add_bitcast_fusion), channel_id=2, replica_groups=mesh['adapter'=64,'tensor'=4] {'adapter'}, dimensions={0}, use_global_device_ids=true | all-gather | bytes 24960 | tf_op jit(solution)/shard_map/all_gather | solution.py:52
  57.1 0.1 select_reduce_fusion.2
  57.3 0.5 broadcast_and_fusion
  57.8 1.5 and.72
  59.3 2.0 convolution_convert_fusion.1
  61.3 6.6 %all-to-all-start.1 = ((bf16[64,16,1024]{2,1,0:T(8,128)(2,1)}), bf16[64,16,1024]{2,1,0:T(8,128)(2,1)S(1)}, u32[]{:S(2)}, u32[]{:S(2)}) async-start(bf16[64,16,1024]{2,1,0:T(8,128)(2,1)} %bitcast.11), calls=%async_computation.2 | async-start | bytes 4194304 | tf_op jit(solution)/shard_map/all_to_all | solution.py:71
  67.9 2.0 convolution_convert_fusion.2
  70.0 49.2 %all-to-all-done.1 = bf16[64,16,1024]{2,1,0:T(8,128)(2,1)S(1)} async-done(((bf16[64,16,1024]{2,1,0:T(8,128)(2,1)}), bf16[64,16,1024]{2,1,0:T(8,128)(2,1)S(1)}, u32[]{:S(2)}, u32[]{:S(2)}) %all-to-all-start.1) | async-done | bytes 2097184 | tf_op jit(solution)/shard_map/all_to_all | solution.py:71
  119.2 6.1 %all-to-all-start = ((bf16[64,16,1024]{2,1,0:T(8,128)(2,1)}), bf16[64,16,1024]{2,1,0:T(8,128)(2,1)}, u32[]{:S(2)}, u32[]{:S(2)}) async-start(bf16[64,16,1024]{2,1,0:T(8,128)(2,1)} %bitcast.7), calls=%async_computation.1 | async-start | bytes 4194304 | tf_op jit(solution)/shard_map/all_to_all | solution.py:72
  125.5 0.1 reduce
  125.6 0.1 convert_reduce_fusion
  125.7 0.1 select_reduce_fusion
  125.9 3.9 %fusion.13 = f32[1024,512]{1,0:T(8,128)} fusion(bf16[1024,1024]{1,0:T(8,128)(2,1)S(1)} %bitcast.57, bf16[512,1024]{1,0:T(8,128)(2,1)} %param.8), kind=kOutput, calls=%fused_computation.47 | convolution fusion | flops 1073741824 | bytes 5242880 | tf_op jit(solution)/shard_map/dot_general | solution.py:75
  129.7 46.8 %all-to-all-done = bf16[64,16,1024]{2,1,0:T(8,128)(2,1)} async-done(((bf16[64,16,1024]{2,1,0:T(8,128)(2,1)}), bf16[64,16,1024]{2,1,0:T(8,128)(2,1)}, u32[]{:S(2)}, u32[]{:S(2)}) %all-to-all-start) | async-done | bytes 2097184 | tf_op jit(solution)/shard_map/all_to_all | solution.py:72
  176.5 3.0 fusion.11
  179.5 0.7 multiply_reduce_fusion
  180.2 13.6 %all-reduce = (bf16[512,16]{0,1:T(8,128)(2,1)S(1)}, bf16[512,16]{0,1:T(8,128)(2,1)S(1)}) all-reduce(bf16[512,16]{0,1:T(8,128)(2,1)S(1)} %get-tuple-element.16, bf16[512,16]{0,1:T(8,128)(2,1)S(1)} %get-tuple-element.15), channel_id=1, replica_groups=mesh['adapter'=64,'tensor'=4] {'tensor'}, use_global_device_ids=true, to_apply=%region_8.9 | all-reduce | flops 16384 | bytes 65536 | tf_op jit(solution)/shard_map/psum | solution.py:14
  193.8 1.2 broadcast_select_fusion
  195.0 2.6 multiply_convert_fusion
  197.6 9.6 %all-to-all-start.3 = ((bf16[64,16,1024]{2,1,0:T(8,128)(2,1)}), bf16[64,16,1024]{2,1,0:T(8,128)(2,1)S(1)}, u32[]{:S(2)}, u32[]{:S(2)}) async-start(bf16[64,16,1024]{2,1,0:T(8,128)(2,1)} %bitcast.58), calls=%async_computation.4 | async-start | bytes 4194304 | tf_op jit(solution)/shard_map/all_to_all | solution.py:97
  207.2 0.2 reduce-scatter.2.cloned.1.call-start
  207.4 9.6 %convolution_convert_fusion = bf16[4096,512]{1,0:T(8,128)(2,1)} fusion(bf16[4096,1024]{1,0:T(8,128)(2,1)} %param.10, bf16[512,1024]{1,0:T(8,128)(2,1)S(1)} %copy-done), kind=kOutput, calls=%fused_computation | convolution fusion | flops 4297064448 | bytes 13631488 | tf_op jit(solution)/shard_map/dot_general | solution.py:117
  217.0 4.2 %multiply_convert_fusion.1 = bf16[1024,1024]{1,0:T(8,128)(2,1)} fusion(bf16[512,1024]{0,1:T(8,128)(2,1)} %bitcast.62, bf16[512,1024]{1,0:T(8,128)(2,1)} %param.8), kind=kOutput, calls=%fused_computation.2 | convolution fusion | flops 1075838976 | bytes 4194304 | tf_op jit(solution)/shard_map/dot_general | solution.py:87
  221.2 37.2 %all-to-all-done.3 = bf16[64,16,1024]{2,1,0:T(8,128)(2,1)S(1)} async-done(((bf16[64,16,1024]{2,1,0:T(8,128)(2,1)}), bf16[64,16,1024]{2,1,0:T(8,128)(2,1)S(1)}, u32[]{:S(2)}, u32[]{:S(2)}) %all-to-all-start.3) | async-done | bytes 2097184 | tf_op jit(solution)/shard_map/all_to_all | solution.py:97
  258.4 6.0 %all-to-all-start.2 = ((bf16[64,16,1024]{2,1,0:T(8,128)(2,1)}), bf16[64,16,1024]{2,1,0:T(8,128)(2,1)}, u32[]{:S(2)}, u32[]{:S(2)}) async-start(bf16[64,16,1024]{2,1,0:T(8,128)(2,1)} %bitcast.59), calls=%async_computation.3 | async-start | bytes 4194304 | tf_op jit(solution)/shard_map/all_to_all | solution.py:94
  264.4 1.3 fusion.14
  265.7 49.9 %all-to-all-done.2 = bf16[64,16,1024]{2,1,0:T(8,128)(2,1)} async-done(((bf16[64,16,1024]{2,1,0:T(8,128)(2,1)}), bf16[64,16,1024]{2,1,0:T(8,128)(2,1)}, u32[]{:S(2)}, u32[]{:S(2)}) %all-to-all-start.2) | async-done | bytes 2097184 | tf_op jit(solution)/shard_map/all_to_all | solution.py:94
  315.6 2.9 fusion.12
  318.5 3.5 %fusion.1 = bf16[512,1024]{0,1:T(8,128)(2,1)} fusion(bf16[1024,512]{1,0:T(8,128)(2,1)} %reduce-scatter.2.cloned.1.call-done, bf16[64,16,1024]{2,1,0:T(8,128)(2,1)S(1)} %copy-done.2, pred[512,64]{0,1:T(8,128)(4,1)S(1)} %get-tuple-element.26, bf16[512,16]{0,1:T(8,128)(2,1)S(1)} %get-tuple-element.19), kind=kOutput, calls=%fused_computation.6 | convolution fusion | flops 1077411840 | bytes 4243456 | tf_op jit(solution)/shard_map/dot_general | solution.py:85
  322.0 2.3 copy.30
  (24 shorter events, 0.4 us)
Async XLA Ops:
  7.2 169.3 %copy-start = (bf16[512,1024]{1,0:T(8,128)(2,1)S(1)}, bf16[512,1024]{1,0:T(8,128)(2,1)}, u32[]{:S(2)}) copy-start(bf16[512,1024]{1,0:T(8,128)(2,1)} %param.9) | copy-start | bytes 3145732
  7.2 52.1 %copy-start.4 = (bf16[128,1024]{1,0:T(8,128)(2,1)S(1)}, bf16[128,1024]{1,0:T(8,128)(2,1)}, u32[]{:S(2)}) copy-start(bf16[128,1024]{1,0:T(8,128)(2,1)} %param.11) | copy-start | bytes 786436
  61.3 6.6 %copy-start.5 = (bf16[128,1024]{1,0:T(8,128)(2,1)S(1)}, bf16[128,1024]{1,0:T(8,128)(2,1)}, u32[]{:S(2)}) copy-start(bf16[128,1024]{1,0:T(8,128)(2,1)} %param.12) | copy-start | bytes 786436
  61.3 57.8 %all-to-all-start.1 = ((bf16[64,16,1024]{2,1,0:T(8,128)(2,1)}), bf16[64,16,1024]{2,1,0:T(8,128)(2,1)S(1)}, u32[]{:S(2)}, u32[]{:S(2)}) async-start(bf16[64,16,1024]{2,1,0:T(8,128)(2,1)} %bitcast.11), calls=%async_computation.2 | async-start | bytes 4194304 | tf_op jit(solution)/shard_map/all_to_all | solution.py:71
  119.2 6.7 %copy-start.1 = (bf16[64,16,1024]{2,1,0:T(8,128)(2,1)}, bf16[64,16,1024]{2,1,0:T(8,128)(2,1)S(1)}, u32[]{:S(2)}) copy-start(bf16[64,16,1024]{2,1,0:T(8,128)(2,1)S(1)} %all-to-all-done.1) | copy-start | bytes 6291460
  119.2 6.1 %copy-start.6 = (s32[1,48]{1,0:T(1,128)S(1)}, s32[1,48]{1,0:T(1,128)}, u32[]{:S(2)}) copy-start(s32[1,48]{1,0:T(1,128)} %param.15) | copy-start | bytes 580
  119.2 57.3 %all-to-all-start = ((bf16[64,16,1024]{2,1,0:T(8,128)(2,1)}), bf16[64,16,1024]{2,1,0:T(8,128)(2,1)}, u32[]{:S(2)}, u32[]{:S(2)}) async-start(bf16[64,16,1024]{2,1,0:T(8,128)(2,1)} %bitcast.7), calls=%async_computation.1 | async-start | bytes 4194304 | tf_op jit(solution)/shard_map/all_to_all | solution.py:72
  176.5 3.0 copy-start.3
  197.6 60.8 %all-to-all-start.3 = ((bf16[64,16,1024]{2,1,0:T(8,128)(2,1)}), bf16[64,16,1024]{2,1,0:T(8,128)(2,1)S(1)}, u32[]{:S(2)}, u32[]{:S(2)}) async-start(bf16[64,16,1024]{2,1,0:T(8,128)(2,1)} %bitcast.58), calls=%async_computation.4 | async-start | bytes 4194304 | tf_op jit(solution)/shard_map/all_to_all | solution.py:97
  207.2 111.3 %reduce-scatter.2.cloned.1.call-start = ((), (), s32[]{:S(2)}) async-start(), calls=%async_computation.5 | async-start | bytes 5242880 | tf_op jit(solution)/shard_map/reduce_scatter | solution.py:116
  258.4 57.2 %all-to-all-start.2 = ((bf16[64,16,1024]{2,1,0:T(8,128)(2,1)}), bf16[64,16,1024]{2,1,0:T(8,128)(2,1)}, u32[]{:S(2)}, u32[]{:S(2)}) async-start(bf16[64,16,1024]{2,1,0:T(8,128)(2,1)} %bitcast.59), calls=%async_computation.3 | async-start | bytes 4194304 | tf_op jit(solution)/shard_map/all_to_all | solution.py:94
  265.7 52.8 %copy-start.2 = (bf16[64,16,1024]{2,1,0:T(8,128)(2,1)S(1)}, bf16[64,16,1024]{2,1,0:T(8,128)(2,1)}, u32[]{:S(2)}) copy-start(bf16[64,16,1024]{2,1,0:T(8,128)(2,1)} %copy-done.1) | copy-start | bytes 6291460
Sparse Core Ops, SparseCore 0:
  217.1 48.8 reduce-scatter.1
where the time goes:
time: 332 us; the launch traced here: 331 us
  waiting for transfers between devices  183 us (55%)
  blocking collectives  61.7 us (19%)
  matrix products  35 us (11%)
  starting transfers between devices  28.5 us (9%)
  between operations  14.2 us (4%)
  other arithmetic  4.68 us (1%)
  local copies, waits for them, and re-layouts  3.91 us (1%)
    all_to_all x1, waiting for transfers between devices, on_device(): lax.all_to_all(partial_down.astype(jnp.bfloat16), 'adapter', split_axis=0...  49.9 us
    all_to_all x1, waiting for transfers between devices, on_device(): lax.all_to_all(outgoing_down, 'adapter', split_axis=0, concat_axis=0, til...  49.2 us
    all_gather x1, blocking collectives, on_device(): lax.all_gather(jnp.stack([group_slot, lengths])[None], 'adapter', axis=0,...  48.1 us
    all_to_all x1, waiting for transfers between devices, on_device(): lax.all_to_all(outgoing_up, 'adapter', split_axis=0, concat_axis=0, tiled...  46.8 us
    all_to_all x1, waiting for transfers between devices, on_device(): lax.all_to_all(partial_up.astype(jnp.bfloat16), 'adapter', split_axis=0,...  37.2 us
    psum x1, blocking collectives, rank_sums(): lax.psum(up_part.astype(jnp.bfloat16), 'tensor').astype(jnp.float32)  13.6 us
    all_to_all x1, starting transfers between devices, on_device(): lax.all_to_all(partial_up.astype(jnp.bfloat16), 'adapter', split_axis=0,...  9.57 us
    dot_general x1, matrix products, on_device(): lax.dot_general(frozen_weight, output_gradient, (((1,), (1,)), ((), ())),...  9.56 us
  transfers between devices with their start and end apart: 5, of which 4 were waited for; matrix products, arithmetic and copies ran while one was open for 7% of the time, Pallas kernels for 0%

commit v1 on v0

--- a/solution.py
+++ b/solution.py
@@ -6,6 +6,12 @@
 ADAPTER_RANK = 16
 ADP_DEV = 8
 adapter_scale = 2.0
+
+
+def order_modes(mat):
+    return jnp.concatenate(
+        lax.all_to_all(jnp.stack(lax.axis_size("adapter") * [mat]), "adapter", 0, 0), axis=0
+    )
 
 
 def rank_sums(down_part, up_part):
@@ -49,7 +55,7 @@
     tok_group = jnp.sum((positions[:, None] >= group_end[None, :]).astype(jnp.int32), axis=1)
     group_onehot = tok_group[:, None] == jnp.arange(lengths.shape[0], dtype=jnp.int32)[None, :]
     tok_owner = jnp.sum(jnp.where(group_onehot, group_owner[None, :], 0), axis=1)
-    gathered = lax.all_gather(jnp.stack([group_slot, lengths])[None], "adapter", axis=0, tiled=True)
+    gathered = order_modes(jnp.stack([group_slot, lengths])[None])
     from_mine = gathered[:, 0] // ADP_DEV == own_index
     source_count = jnp.sum(jnp.where(from_mine, gathered[:, 1], 0), axis=1)
     source_local = jnp.sum(jnp.where(from_mine, gathered[:, 0] % ADP_DEV, 0), axis=1)

time: 332 us -> 305 us (0.919)
  blocking collectives: 61.7 us -> 13.6 us
  starting transfers between devices: 28.5 us -> 39.6 us
  waiting for transfers between devices: 183 us -> 193 us
    all_gather x1 -> x0, blocking collectives: 48.1 us -> none  [on_device(): lax.all_gather(jnp.stack([group_slot, lengths])[None], 'adapter', axis=0,...]
    all_to_all x0 -> x1, starting transfers between devices: none -> 13 us  [order_modes(): lax.all_to_all(jnp.stack(lax.axis_size('adapter') * [mat]), 'adapter', 0, 0)]
    all_to_all x0 -> x1, waiting for transfers between devices: none -> 9.77 us  [order_modes(): lax.all_to_all(jnp.stack(lax.axis_size('adapter') * [mat]), 'adapter', 0, 0)]
  transfers between devices with their start and end apart: 5 -> 6, of which waited for: 4 -> 5; matrix products, arithmetic and copies ran while one was open for 7% -> 8% of each run, Pallas kernels for 0% -> 0%
where the time goes in v1:
time: 305 us
  waiting for transfers between devices  193 us (63%)
  starting transfers between devices  39.6 us (13%)
  matrix products  35 us (11%)
  between operations  14.2 us (5%)
  blocking collectives  13.6 us (4%)
  other arithmetic  4.68 us (2%)
  local copies, waits for them, and re-layouts  4.56 us (1%)
    all_to_all x1, waiting for transfers between devices, on_device(): lax.all_to_all(partial_down.astype(jnp.bfloat16), 'adapter', split_axis=0...  49.9 us
    all_to_all x1, waiting for transfers between devices, on_device(): lax.all_to_all(outgoing_down, 'adapter', split_axis=0, concat_axis=0, til...  49.3 us
    all_to_all x1, waiting for transfers between devices, on_device(): lax.all_to_all(outgoing_up, 'adapter', split_axis=0, concat_axis=0, tiled...  46.8 us
    all_to_all x1, waiting for transfers between devices, on_device(): lax.all_to_all(partial_up.astype(jnp.bfloat16), 'adapter', split_axis=0,...  37.2 us
    psum x1, blocking collectives, rank_sums(): lax.psum(up_part.astype(jnp.bfloat16), 'tensor').astype(jnp.float32)  13.6 us
    all_to_all x1, starting transfers between devices, order_modes(): lax.all_to_all(jnp.stack(lax.axis_size('adapter') * [mat]), 'adapter', 0, 0)  13 us
    all_to_all x1, waiting for transfers between devices, order_modes(): lax.all_to_all(jnp.stack(lax.axis_size('adapter') * [mat]), 'adapter', 0, 0)  9.77 us
    all_to_all x1, starting transfers between devices, on_device(): lax.all_to_all(partial_up.astype(jnp.bfloat16), 'adapter', split_axis=0,...  9.57 us
  transfers between devices with their start and end apart: 6, of which 5 were waited for; matrix products, arithmetic and copies ran while one was open for 8% of the time, Pallas kernels for 0%

profile of v1, /device:TPU:1, one launch (start us, length us, event | category | flops | bytes accessed | tf_op | source)
XLA Modules:
  0.0 304.6 jit_solution(9300123994571639739)
XLA Ops:
  7.2 1.0 select_reduce_fusion.1
  8.2 0.7 pad_add_fusion
  8.8 0.6 stack.8
  9.5 13.0 %all-to-all-start = ((s32[64,1,2,48]{3,2,1,0:T(2,128)}), s32[64,1,2,48]{3,2,1,0:T(2,128)S(1)}, u32[]{:S(2)}, u32[]{:S(2)}) async-start(s32[64,1,2,48]{3,2,1,0:T(2,128)} %stack.8), calls=%async_computation.1 | async-start | bytes 131072 | tf_op jit(solution)/shard_map/all_to_all | solution.py:13
  22.5 9.8 %all-to-all-done = s32[64,1,2,48]{3,2,1,0:T(2,128)S(1)} async-done(((s32[64,1,2,48]{3,2,1,0:T(2,128)}), s32[64,1,2,48]{3,2,1,0:T(2,128)S(1)}, u32[]{:S(2)}, u32[]{:S(2)}) %all-to-all-start) | async-done | bytes 24608 | tf_op jit(solution)/shard_map/all_to_all | solution.py:13
  32.3 0.1 select_reduce_fusion.2
  32.6 0.5 broadcast_and_fusion
  33.1 1.5 and.72
  34.6 2.0 convolution_convert_fusion.1
  36.6 4.7 %all-to-all-start.2 = ((bf16[64,16,1024]{2,1,0:T(8,128)(2,1)}), bf16[64,16,1024]{2,1,0:T(8,128)(2,1)S(1)}, u32[]{:S(2)}, u32[]{:S(2)}) async-start(bf16[64,16,1024]{2,1,0:T(8,128)(2,1)} %bitcast.11), calls=%async_computation.3 | async-start | bytes 4194304 | tf_op jit(solution)/shard_map/all_to_all | solution.py:77
  41.3 2.0 convolution_convert_fusion.2
  43.3 49.3 %all-to-all-done.2 = bf16[64,16,1024]{2,1,0:T(8,128)(2,1)S(1)} async-done(((bf16[64,16,1024]{2,1,0:T(8,128)(2,1)}), bf16[64,16,1024]{2,1,0:T(8,128)(2,1)S(1)}, u32[]{:S(2)}, u32[]{:S(2)}) %all-to-all-start.2) | async-done | bytes 2097184 | tf_op jit(solution)/shard_map/all_to_all | solution.py:77
  92.6 6.1 %all-to-all-start.1 = ((bf16[64,16,1024]{2,1,0:T(8,128)(2,1)}), bf16[64,16,1024]{2,1,0:T(8,128)(2,1)}, u32[]{:S(2)}, u32[]{:S(2)}) async-start(bf16[64,16,1024]{2,1,0:T(8,128)(2,1)} %bitcast.7), calls=%async_computation.2 | async-start | bytes 4194304 | tf_op jit(solution)/shard_map/all_to_all | solution.py:78
  98.9 0.1 reduce
  99.3 3.9 %fusion.13 = f32[1024,512]{1,0:T(8,128)} fusion(bf16[1024,1024]{1,0:T(8,128)(2,1)S(1)} %bitcast.56, bf16[512,1024]{1,0:T(8,128)(2,1)} %param.8), kind=kOutput, calls=%fused_computation.47 | convolution fusion | flops 1073741824 | bytes 5242880 | tf_op jit(solution)/shard_map/dot_general | solution.py:81
  103.2 46.8 %all-to-all-done.1 = bf16[64,16,1024]{2,1,0:T(8,128)(2,1)} async-done(((bf16[64,16,1024]{2,1,0:T(8,128)(2,1)}), bf16[64,16,1024]{2,1,0:T(8,128)(2,1)}, u32[]{:S(2)}, u32[]{:S(2)}) %all-to-all-start.1) | async-done | bytes 2097184 | tf_op jit(solution)/shard_map/all_to_all | solution.py:78
  149.9 3.0 fusion.11
  153.0 0.7 multiply_reduce_fusion
  153.6 13.6 %all-reduce = (bf16[512,16]{0,1:T(8,128)(2,1)S(1)}, bf16[512,16]{0,1:T(8,128)(2,1)S(1)}) all-reduce(bf16[512,16]{0,1:T(8,128)(2,1)S(1)} %get-tuple-element.19, bf16[512,16]{0,1:T(8,128)(2,1)S(1)} %get-tuple-element.18), channel_id=1, replica_groups=mesh['adapter'=64,'tensor'=4] {'tensor'}, use_global_device_ids=true, to_apply=%region_8.9 | all-reduce | flops 16384 | bytes 65536 | tf_op jit(solution)/shard_map/psum | solution.py:20
  167.2 1.2 broadcast_select_fusion
  168.4 2.6 multiply_convert_fusion
  171.0 9.6 %all-to-all-start.4 = ((bf16[64,16,1024]{2,1,0:T(8,128)(2,1)}), bf16[64,16,1024]{2,1,0:T(8,128)(2,1)S(1)}, u32[]{:S(2)}, u32[]{:S(2)}) async-start(bf16[64,16,1024]{2,1,0:T(8,128)(2,1)} %bitcast.57), calls=%async_computation.5 | async-start | bytes 4194304 | tf_op jit(solution)/shard_map/all_to_all | solution.py:103
  180.6 0.2 reduce-scatter.2.cloned.1.call-start
  180.8 9.6 %convolution_convert_fusion = bf16[4096,512]{1,0:T(8,128)(2,1)} fusion(bf16[4096,1024]{1,0:T(8,128)(2,1)} %param.10, bf16[512,1024]{1,0:T(8,128)(2,1)S(1)} %copy-done), kind=kOutput, calls=%fused_computation | convolution fusion | flops 4297064448 | bytes 13631488 | tf_op jit(solution)/shard_map/dot_general | solution.py:123
  190.4 4.2 %multiply_convert_fusion.1 = bf16[1024,1024]{1,0:T(8,128)(2,1)} fusion(bf16[512,1024]{0,1:T(8,128)(2,1)} %bitcast.61, bf16[512,1024]{1,0:T(8,128)(2,1)} %param.8), kind=kOutput, calls=%fused_computation.2 | convolution fusion | flops 1075838976 | bytes 4194304 | tf_op jit(solution)/shard_map/dot_general | solution.py:93
  194.6 37.2 %all-to-all-done.4 = bf16[64,16,1024]{2,1,0:T(8,128)(2,1)S(1)} async-done(((bf16[64,16,1024]{2,1,0:T(8,128)(2,1)}), bf16[64,16,1024]{2,1,0:T(8,128)(2,1)S(1)}, u32[]{:S(2)}, u32[]{:S(2)}) %all-to-all-start.4) | async-done | bytes 2097184 | tf_op jit(solution)/shard_map/all_to_all | solution.py:103
  231.8 6.0 %all-to-all-start.3 = ((bf16[64,16,1024]{2,1,0:T(8,128)(2,1)}), bf16[64,16,1024]{2,1,0:T(8,128)(2,1)}, u32[]{:S(2)}, u32[]{:S(2)}) async-start(bf16[64,16,1024]{2,1,0:T(8,128)(2,1)} %bitcast.58), calls=%async_computation.4 | async-start | bytes 4194304 | tf_op jit(solution)/shard_map/all_to_all | solution.py:100
  237.9 1.3 fusion.14
  239.2 49.9 %all-to-all-done.3 = bf16[64,16,1024]{2,1,0:T(8,128)(2,1)} async-done(((bf16[64,16,1024]{2,1,0:T(8,128)(2,1)}), bf16[64,16,1024]{2,1,0:T(8,128)(2,1)}, u32[]{:S(2)}, u32[]{:S(2)}) %all-to-all-start.3) | async-done | bytes 2097184 | tf_op jit(solution)/shard_map/all_to_all | solution.py:100
  289.0 2.9 fusion.12
  291.9 3.5 %fusion.1 = bf16[512,1024]{0,1:T(8,128)(2,1)} fusion(bf16[1024,512]{1,0:T(8,128)(2,1)} %reduce-scatter.2.cloned.1.call-done, bf16[64,16,1024]{2,1,0:T(8,128)(2,1)S(1)} %copy-done.2, pred[512,64]{0,1:T(8,128)(4,1)S(1)} %get-tuple-element.29, bf16[512,16]{0,1:T(8,128)(2,1)S(1)} %get-tuple-element.22), kind=kOutput, calls=%fused_computation.6 | convolution fusion | flops 1077411840 | bytes 4243456 | tf_op jit(solution)/shard_map/dot_general | solution.py:91
  295.4 2.3 copy.35
  (26 shorter events, 0.6 us)
Async XLA Ops:
  7.2 142.8 %copy-start = (bf16[512,1024]{1,0:T(8,128)(2,1)S(1)}, bf16[512,1024]{1,0:T(8,128)(2,1)}, u32[]{:S(2)}) copy-start(bf16[512,1024]{1,0:T(8,128)(2,1)} %param.9) | copy-start | bytes 3145732
  7.2 27.4 %copy-start.4 = (bf16[128,1024]{1,0:T(8,128)(2,1)S(1)}, bf16[128,1024]{1,0:T(8,128)(2,1)}, u32[]{:S(2)}) copy-start(bf16[128,1024]{1,0:T(8,128)(2,1)} %param.11) | copy-start | bytes 786436
  9.5 22.8 %all-to-all-start = ((s32[64,1,2,48]{3,2,1,0:T(2,128)}), s32[64,1,2,48]{3,2,1,0:T(2,128)S(1)}, u32[]{:S(2)}, u32[]{:S(2)}) async-start(s32[64,1,2,48]{3,2,1,0:T(2,128)} %stack.8), calls=%async_computation.1 | async-start | bytes 131072 | tf_op jit(solution)/shard_map/all_to_all | solution.py:13
  36.6 4.7 %copy-start.5 = (bf16[128,1024]{1,0:T(8,128)(2,1)S(1)}, bf16[128,1024]{1,0:T(8,128)(2,1)}, u32[]{:S(2)}) copy-start(bf16[128,1024]{1,0:T(8,128)(2,1)} %param.12) | copy-start | bytes 786436
  36.6 56.0 %all-to-all-start.2 = ((bf16[64,16,1024]{2,1,0:T(8,128)(2,1)}), bf16[64,16,1024]{2,1,0:T(8,128)(2,1)S(1)}, u32[]{:S(2)}, u32[]{:S(2)}) async-start(bf16[64,16,1024]{2,1,0:T(8,128)(2,1)} %bitcast.11), calls=%async_computation.3 | async-start | bytes 4194304 | tf_op jit(solution)/shard_map/all_to_all | solution.py:77
  92.6 6.7 %copy-start.1 = (bf16[64,16,1024]{2,1,0:T(8,128)(2,1)}, bf16[64,16,1024]{2,1,0:T(8,128)(2,1)S(1)}, u32[]{:S(2)}) copy-start(bf16[64,16,1024]{2,1,0:T(8,128)(2,1)S(1)} %all-to-all-done.2) | copy-start | bytes 6291460
  92.6 6.1 %copy-start.6 = (s32[1,48]{1,0:T(1,128)S(1)}, s32[1,48]{1,0:T(1,128)}, u32[]{:S(2)}) copy-start(s32[1,48]{1,0:T(1,128)} %param.15) | copy-start | bytes 580
  92.6 57.3 %all-to-all-start.1 = ((bf16[64,16,1024]{2,1,0:T(8,128)(2,1)}), bf16[64,16,1024]{2,1,0:T(8,128)(2,1)}, u32[]{:S(2)}, u32[]{:S(2)}) async-start(bf16[64,16,1024]{2,1,0:T(8,128)(2,1)} %bitcast.7), calls=%async_computation.2 | async-start | bytes 4194304 | tf_op jit(solution)/shard_map/all_to_all | solution.py:78
  149.9 3.0 copy-start.3
  171.0 60.8 %all-to-all-start.4 = ((bf16[64,16,1024]{2,1,0:T(8,128)(2,1)}), bf16[64,16,1024]{2,1,0:T(8,128)(2,1)S(1)}, u32[]{:S(2)}, u32[]{:S(2)}) async-start(bf16[64,16,1024]{2,1,0:T(8,128)(2,1)} %bitcast.57), calls=%async_computation.5 | async-start | bytes 4194304 | tf_op jit(solution)/shard_map/all_to_all | solution.py:103
  180.6 111.3 %reduce-scatter.2.cloned.1.call-start = ((), (), s32[]{:S(2)}) async-start(), calls=%async_computation.6 | async-start | bytes 5242880 | tf_op jit(solution)/shard_map/reduce_scatter | solution.py:122
  231.8 57.2 %all-to-all-start.3 = ((bf16[64,16,1024]{2,1,0:T(8,128)(2,1)}), bf16[64,16,1024]{2,1,0:T(8,128)(2,1)}, u32[]{:S(2)}, u32[]{:S(2)}) async-start(bf16[64,16,1024]{2,1,0:T(8,128)(2,1)} %bitcast.58), calls=%async_computation.4 | async-start | bytes 4194304 | tf_op jit(solution)/shard_map/all_to_all | solution.py:100
  239.2 52.8 %copy-start.2 = (bf16[64,16,1024]{2,1,0:T(8,128)(2,1)S(1)}, bf16[64,16,1024]{2,1,0:T(8,128)(2,1)}, u32[]{:S(2)}) copy-start(bf16[64,16,1024]{2,1,0:T(8,128)(2,1)} %copy-done.1) | copy-start | bytes 6291460
Sparse Core Ops, SparseCore 0:
  190.5 48.8 reduce-scatter.1
